TPU v7x, 32 devices: a whole 2x2x4 slice. The times are simulated.
32 devices in a mesh: grp: 8 (over z, core), col: 4 (over y, x).
Axes of the slice: x: 2, y: 2, z: 4, core: 2. Of those that a mesh axis runs over, the one named last changes fastest.
Arguments:
- constraint_rows: float32 [2048, 16384], P('grp', 'col'), may hold values from -0.1875 to 0.1875
- shift: float32 [16384], P('col'), may hold values from 0.3 to 1
- group_rows: int32 [8], replicated, may hold values from 1 to 256, 1024 in all
- panel_index: int32 [1], replicated, may hold values from 0 to 31
Outputs:
- panel_factor: float32 [16384, 512], P(('col', 'grp'))
Inputs may be any that keep to these rules, and one draw needn't show every extreme that they name: `group_rows`: the values sum to 1024 and the largest equals 256.
All inputs are finite; a program needn't handle non-finite values.
Results may differ from a plain program's by a relative error of at most 0.000076.
Values sent between devices are 32-bit elements; how exact they have to be, the bound alone decides.
No kernel may reach another device: no remote copies, remote signals or barrier semaphores. Data moves between devices by JAX's collectives and lax.ppermute only.
A program may use at most 64 MiB of HBM per device.

v0:
```python
import jax
import jax.numpy as jnp
from jax import lax
from jax.sharding import PartitionSpec as P

PANEL = 512


def spread(value, axis, source):
    kept = jnp.where(lax.axis_index(axis) == source, value, 0).astype(value.dtype)
    return lax.psum(kept, axis)


def product(left, right):
    return lax.dot_general(
        left,
        right,
        (((0,), (0,)), ((), ())),
        precision=lax.Precision.HIGHEST,
        preferred_element_type=jnp.float32,
    )


def gram_rows(left, panel_cols):
    return product(left, panel_cols)


def add_shift(values, shift_part, first_row, start):
    row_ids = first_row + jnp.arange(values.shape[0], dtype=jnp.int32)
    col_ids = jnp.arange(values.shape[1], dtype=jnp.int32)
    on_diag = row_ids[:, None] == start + col_ids[None, :]
    return values + jnp.where(on_diag, shift_part[:, None], jnp.zeros_like(values))


def on_device(constraint_rows, shift, group_rows, panel_index):
    width = constraint_rows.shape[1]
    groups = lax.axis_size("grp")
    col_idx = lax.axis_index("col")
    grp_idx = lax.axis_index("grp")
    share = width // groups
    start = panel_index[0] * PANEL
    owner = start // width
    local = start - owner * width
    live_count = lax.dynamic_index_in_dim(group_rows, grp_idx, keepdims=False)
    row_ids = jnp.arange(constraint_rows.shape[0], dtype=jnp.int32)
    masked = jnp.where(
        (row_ids < live_count)[:, None], constraint_rows, jnp.zeros_like(constraint_rows)
    )
    own_cols = lax.dynamic_slice_in_dim(masked, local, PANEL, 1)
    panel_cols = spread(own_cols, "col", owner)
    mine = lax.psum_scatter(gram_rows(masked, panel_cols), "grp", scatter_dimension=0, tiled=True)
    shift_part = lax.dynamic_slice_in_dim(shift, grp_idx * share, share, 0)
    mine = add_shift(mine, shift_part, col_idx * width + grp_idx * share, start)
    from_owner = spread(mine, "col", owner)
    owner_shard = lax.all_gather(from_owner, "grp", axis=0, tiled=True)
    block = lax.dynamic_slice_in_dim(owner_shard, local, PANEL, 0)
    factor = jnp.linalg.cholesky(block)
    return lax.linalg.triangular_solve(factor, mine, left_side=False, lower=True, transpose_a=True)


def solution(mesh):
    placed = (P("grp", "col"), P("col"), P(), P())
    return jax.shard_map(
        on_device, mesh=mesh, in_specs=placed, out_specs=P(("col", "grp"), None), check_vma=False
    )
```

profile of v0, /device:TPU:0, one launch (start us, length us, event | category | flops | bytes accessed | tf_op | source)
XLA Modules:
  0.0 456.2 jit_solution(14279426750491171886)
XLA Ops:
  9.1 2.7 broadcast_select_fusion
  11.8 2.0 copy-done
  14.7 48.2 %all-reduce.4.cloned.1.call-done = f32[256,512]{1,0:T(8,128)} async-done(((f32[256,512]{1,0:T(8,128)}), f32[256,512]{1,0:T(8,128)}) %all-reduce.4.cloned.1.call-update) | async-done | bytes 524304 | tf_op jit(solution)/shard_map/psum | solution.py:11
  62.9 10.9 %fusion.31 = f32[4096,512]{0,1:T(8,128)} fusion(f32[256,4096]{1,0:T(8,128)} %copy-done, f32[256,512]{1,0:T(8,128)} %all-reduce.4.cloned.1.call-done), kind=kOutput, calls=%fused_computation.75 | convolution fusion | flops 6442450944 | bytes 13107200 | tf_op jit(solution)/shard_map/dot_general | solution.py:15
  74.6 88.9 %reduce-scatter.2.cloned.1.call-done = f32[512,512]{0,1:T(8,128)} async-done(((f32[4096,512]{0,1:T(8,128)}), f32[512,512]{0,1:T(8,128)}) %reduce-scatter.2.cloned.1.call-update) | async-done | bytes 1048592 | tf_op jit(solution)/shard_map/reduce_scatter | solution.py:51
  163.4 2.4 broadcast_select_fusion.1
  166.1 51.4 %all-reduce.6.cloned.1.call-done = f32[512,512]{0,1:T(8,128)} async-done(((f32[512,512]{0,1:T(8,128)}), f32[512,512]{0,1:T(8,128)}) %all-reduce.6.cloned.1.call-update) | async-done | bytes 1048592 | tf_op jit(solution)/shard_map/psum | solution.py:11
  217.5 83.5 %all-gather.2.cloned.1.call-done = f32[4096,512]{0,1:T(8,128)} async-done(((f32[512,512]{0,1:T(8,128)}), f32[4096,512]{0,1:T(8,128)}) %all-gather.2.cloned.1.call-update) | async-done | bytes 8388624 | tf_op jit(solution)/shard_map/all_gather | solution.py:55
  301.0 1.3 constant_dynamic-slice_fusion.1
  302.7 1.5 fusion
  304.1 11.7 %cholesky.103 = f32[128,128]{1,0:T(8,128)S(1)} custom-call(f32[128,128]{1,0:T(8,128)S(1)} %cholesky.263), custom_call_target="Cholesky" | custom-call | tf_op jit(solution)/shard_map/jit(cholesky)/cholesky | solution.py:57
  315.9 9.8 %custom-call.30 = f32[1,128,128]{1,2,0:T(8,128)S(1)} custom-call(f32[1,128,128]{2,1,0:T(8,128)S(1)} %get-tuple-element.34), custom_call_target="InvertDiagBlocksLowerTriangular" | custom-call | tf_op jit(solution)/shard_map/jit(cholesky)/cholesky | solution.py:57
  326.4 11.7 %cholesky.215 = f32[128,128]{1,0:T(8,128)S(1)} custom-call(f32[128,128]{1,0:T(8,128)S(1)} %cholesky.267), custom_call_target="Cholesky" | custom-call | tf_op jit(solution)/shard_map/jit(cholesky)/cholesky | solution.py:57
  339.7 10.6 %custom-call.31 = f32[1,128,128]{1,2,0:T(8,128)} custom-call(f32[1,128,128]{2,1,0:T(8,128)S(1)} %get-tuple-element.32), custom_call_target="InvertDiagBlocksLowerTriangular" | custom-call | tf_op jit(solution)/shard_map/jit(cholesky)/cholesky | solution.py:57
  353.9 11.7 %cholesky.236 = f32[128,128]{1,0:T(8,128)S(1)} custom-call(f32[128,128]{1,0:T(8,128)S(1)} %cholesky.272), custom_call_target="Cholesky" | custom-call | tf_op jit(solution)/shard_map/jit(cholesky)/cholesky | solution.py:57
  365.8 9.8 %custom-call.32 = f32[1,128,128]{1,2,0:T(8,128)S(1)} custom-call(f32[1,128,128]{2,1,0:T(8,128)S(1)} %get-tuple-element.30), custom_call_target="InvertDiagBlocksLowerTriangular" | custom-call | tf_op jit(solution)/shard_map/jit(cholesky)/cholesky | solution.py:57
  376.4 11.9 %cholesky.253 = f32[128,128]{1,0:T(8,128)S(1)} custom-call(f32[128,128]{1,0:T(8,128)S(1)} %convolution_subtract_fusion.5), custom_call_target="Cholesky" | custom-call | tf_op jit(solution)/shard_map/jit(cholesky)/cholesky | solution.py:57
  393.8 11.0 %while.1 = (s32[]{:T(128)}, f32[512,512]{0,1:T(8,128)S(1)}, s32[4,2]{0,1:T(2,128)S(1)}, f32[4,128,128]{2,1,0:T(8,128)}, s32[]{:T(128)}) while((s32[]{:T(128)}, f32[512,512]{0,1:T(8,128)S(1)}, s32[4,2]{0,1:T(2,128)S(1)}, f32[4,128,128]{2,1,0:T(8,128)}, s32[]{:T(128)}) %tuple.25), condition=%wide.while_cond, body=%wide.while_body.sunk | while | flops 2 | bytes 393829 | solution.py:58
  394.5 1.3 dynamic-slice.7
  397.3 1.3 dynamic-slice.7
  400.0 1.3 dynamic-slice.7
  402.8 1.3 dynamic-slice.7
  404.9 40.1 %custom-call.33 = f32[4,128,128]{1,2,0:T(8,128)S(1)} custom-call(f32[4,128,128]{2,1,0:T(8,128)} %get-tuple-element.12), custom_call_target="InvertDiagBlocksLowerTriangular" | custom-call | tf_op jit(solution)/shard_map/triangular_solve | solution.py:58
  448.4 1.3 copy.15
  (70 shorter events, 22.9 us)
Async XLA Ops:
  6.5 56.3 %all-reduce.4.cloned.1.call-start = ((), (), s32[]{:S(2)}) async-start(), calls=%async_computation.1 | async-start | bytes 1048576 | tf_op jit(solution)/shard_map/psum | solution.py:11
  11.8 2.0 copy-start
  14.6 148.8 %reduce-scatter.2.cloned.1.call-start = ((), (), s32[]{:S(2)}) async-start(), calls=%async_computation.2 | async-start | bytes 9437184 | tf_op jit(solution)/shard_map/reduce_scatter | solution.py:51
  73.8 143.7 %all-reduce.6.cloned.1.call-start = ((), (), s32[]{:S(2)}) async-start(), calls=%async_computation.3 | async-start | bytes 2097152 | tf_op jit(solution)/shard_map/psum | solution.py:11
  165.9 135.2 %all-gather.2.cloned.1.call-start = ((), (), s32[]{:S(2)}) async-start(), calls=%async_computation.4 | async-start | bytes 9437184 | tf_op jit(solution)/shard_map/all_gather | solution.py:55
Sparse Core Ops, SparseCore 0:
  14.8 48.0 all-reduce.3
  73.9 89.5 reduce-scatter.1
  166.5 50.9 all-reduce.5
  219.0 82.0 all-gather.1
where the time goes:
time: 457 us; the launch traced here: 456 us
  waiting for transfers between devices  272 us (60%)
  other arithmetic  128 us (28%)
  local copies, waits for them, and re-layouts  21.5 us (5%)
  matrix products  17.3 us (4%)
  between operations  16.6 us (4%)
    psum x2, waiting for transfers between devices, spread(): return lax.psum(kept, axis)  99.6 us
    reduce_scatter x1, waiting for transfers between devices, on_device(): lax.psum_scatter(gram_rows(masked, panel_cols), 'grp', scatter_dimension=...  88.9 us
    all_gather x1, waiting for transfers between devices, on_device(): owner_shard = lax.all_gather(from_owner, 'grp', axis=0, tiled=True)  83.5 us
    another operation x15, other arithmetic, on_device(): factor = jnp.linalg.cholesky(block)  80.1 us
    another operation x4, other arithmetic, on_device(): lax.linalg.triangular_solve(factor, mine, left_side=False, lower=True, tr...  40.3 us
    another operation x20, local copies, waits for them, and re-layouts  11 us
    dot_general x1, matrix products, product(): lax.dot_general(left, right, (((0,), (0,)), ((), ())), precision=lax.Prec...  10.9 us
  transfers between devices with their start and end apart: 4, of which 4 were waited for; matrix products, arithmetic and copies ran while one was open for 0% of the time, Pallas kernels for 0%

commit v1 on v0

--- a/solution.py
+++ b/solution.py
@@ -8,7 +8,7 @@
 
 def spread(value, axis, source):
     kept = jnp.where(lax.axis_index(axis) == source, value, 0).astype(value.dtype)
-    return lax.psum(kept, axis)
+    return jnp.sum(lax.all_gather(kept, axis), axis=0)
 
 
 def product(left, right):

time: 457 us -> 452 us (0.989)
  waiting for transfers between devices: 272 us -> 260 us
    psum x2 -> x0, waiting for transfers between devices: 99.6 us -> none  [spread(): return lax.psum(kept, axis)]
    all_gather x0 -> x2, waiting for transfers between devices: none -> 88.7 us  [spread(): return jnp.sum(lax.all_gather(kept, axis), axis=0)]
    reduce_sum x0 -> x2, other arithmetic: none -> 4.64 us  [spread(): return jnp.sum(lax.all_gather(kept, axis), axis=0)]
    another operation x20 -> x12, local copies, waits for them, and re-layouts: 11 us -> 8.39 us
where the time goes in v1:
time: 452 us; the launch traced here: 447 us
  waiting for transfers between devices  260 us (58%)
  other arithmetic  131 us (29%)
  matrix products  20.7 us (5%)
  local copies, waits for them, and re-layouts  17.7 us (4%)
  between operations  17 us (4%)
    reduce_scatter x1, waiting for transfers between devices, on_device(): lax.psum_scatter(gram_rows(masked, panel_cols), 'grp', scatter_dimension=...  88.9 us
    all_gather x2, waiting for transfers between devices, spread(): return jnp.sum(lax.all_gather(kept, axis), axis=0)  88.7 us
    all_gather x1, waiting for transfers between devices, on_device(): owner_shard = lax.all_gather(from_owner, 'grp', axis=0, tiled=True)  82.2 us
    another operation x15, other arithmetic, on_device(): factor = jnp.linalg.cholesky(block)  79.3 us
    another operation x4, other arithmetic, on_device(): lax.linalg.triangular_solve(factor, mine, left_side=False, lower=True, tr...  39.5 us
    dot_general x1, matrix products, product(): lax.dot_general(left, right, (((0,), (0,)), ((), ())), precision=lax.Prec...  10.5 us
  transfers between devices with their start and end apart: 4, of which 4 were waited for; matrix products, arithmetic and copies ran while one was open for 0% of the time, Pallas kernels for 0%

profile of v1, /device:TPU:0, one launch (start us, length us, event | category | flops | bytes accessed | tf_op | source)
XLA Modules:
  0.0 447.3 jit_solution(16408479867956545055)
XLA Ops:
  9.1 2.7 broadcast_select_fusion
  11.8 2.0 copy-done
  14.7 38.0 %all-gather.8.cloned.1.call-done = f32[1024,512]{1,0:T(8,128)} async-done(((f32[256,512]{1,0:T(8,128)}), f32[1024,512]{1,0:T(8,128)}) %all-gather.8.cloned.1.call-update) | async-done | bytes 2097168 | tf_op jit(solution)/shard_map/all_gather | solution.py:11
  52.7 1.9 reduce_sum.18
  54.6 10.5 %fusion.31 = f32[4096,512]{1,0:T(8,128)} fusion(f32[256,4096]{1,0:T(8,128)} %copy-done, f32[256,512]{1,0:T(8,128)S(1)} %reduce_sum.18), kind=kOutput, calls=%fused_computation.75 | convolution fusion | flops 6442450944 | bytes 13107200 | tf_op jit(solution)/shard_map/dot_general | solution.py:15
  65.9 88.9 %reduce-scatter.2.cloned.1.call-done = f32[512,512]{1,0:T(8,128)} async-done(((f32[4096,512]{1,0:T(8,128)}), f32[512,512]{1,0:T(8,128)}) %reduce-scatter.2.cloned.1.call-update) | async-done | bytes 1048592 | tf_op jit(solution)/shard_map/reduce_scatter | solution.py:51
  154.8 2.4 broadcast_select_fusion.1
  157.8 50.7 %all-gather.10.cloned.1.call-done = f32[2048,512]{1,0:T(8,128)} async-done(((f32[512,512]{1,0:T(8,128)}), f32[2048,512]{1,0:T(8,128)}) %all-gather.10.cloned.1.call-update) | async-done | bytes 4194320 | tf_op jit(solution)/shard_map/all_gather | solution.py:11
  208.4 2.8 reduce_sum.19
  212.5 82.2 %all-gather.6.cloned.1.call-done = f32[4096,512]{0,1:T(8,128)} async-done(((f32[512,512]{0,1:T(8,128)}), f32[4096,512]{0,1:T(8,128)}) %all-gather.6.cloned.1.call-update) | async-done | bytes 8388624 | tf_op jit(solution)/shard_map/all_gather | solution.py:55
  296.3 1.5 fusion
  298.8 11.7 %cholesky.103 = f32[128,128]{1,0:T(8,128)S(1)} custom-call(f32[128,128]{1,0:T(8,128)S(1)} %cholesky.263), custom_call_target="Cholesky" | custom-call | tf_op jit(solution)/shard_map/jit(cholesky)/cholesky | solution.py:57
  310.7 9.8 %custom-call.30 = f32[1,128,128]{1,2,0:T(8,128)S(1)} custom-call(f32[1,128,128]{2,1,0:T(8,128)S(1)} %get-tuple-element.34), custom_call_target="InvertDiagBlocksLowerTriangular" | custom-call | tf_op jit(solution)/shard_map/jit(cholesky)/cholesky | solution.py:57
  323.0 11.7 %cholesky.215 = f32[128,128]{1,0:T(8,128)S(1)} custom-call(f32[128,128]{1,0:T(8,128)S(1)} %cholesky.267), custom_call_target="Cholesky" | custom-call | tf_op jit(solution)/shard_map/jit(cholesky)/cholesky | solution.py:57
  336.2 9.8 %custom-call.31 = f32[1,128,128]{1,2,0:T(8,128)S(1)} custom-call(f32[1,128,128]{2,1,0:T(8,128)S(1)} %get-tuple-element.31), custom_call_target="InvertDiagBlocksLowerTriangular" | custom-call | tf_op jit(solution)/shard_map/jit(cholesky)/cholesky | solution.py:57
  347.6 11.7 %cholesky.236 = f32[128,128]{1,0:T(8,128)S(1)} custom-call(f32[128,128]{1,0:T(8,128)S(1)} %cholesky.272), custom_call_target="Cholesky" | custom-call | tf_op jit(solution)/shard_map/jit(cholesky)/cholesky | solution.py:57
  360.0 9.8 %custom-call.32 = f32[1,128,128]{1,2,0:T(8,128)S(1)} custom-call(f32[1,128,128]{2,1,0:T(8,128)S(1)} %get-tuple-element.28), custom_call_target="InvertDiagBlocksLowerTriangular" | custom-call | tf_op jit(solution)/shard_map/jit(cholesky)/cholesky | solution.py:57
  371.3 11.9 %cholesky.253 = f32[128,128]{1,0:T(8,128)S(1)} custom-call(f32[128,128]{1,0:T(8,128)S(1)} %convolution_subtract_fusion.5), custom_call_target="Cholesky" | custom-call | tf_op jit(solution)/shard_map/jit(cholesky)/cholesky | solution.py:57
  386.6 8.5 %while.1 = (s32[]{:T(128)}, f32[512,512]{1,0:T(8,128)S(1)}, s32[4,2]{0,1:T(2,128)S(1)}, f32[4,128,128]{2,1,0:T(8,128)S(1)}, s32[]{:T(128)}) while((s32[]{:T(128)}, f32[512,512]{1,0:T(8,128)S(1)}, s32[4,2]{0,1:T(2,128)S(1)}, f32[4,128,128]{2,1,0:T(8,128)S(1)}, s32[]{:T(128)}) %tuple.28), condition=%wide.while_cond, body=%wide.while_body.sunk | while | flops 2 | bytes 131181 | solution.py:58
  387.2 1.4 bitcast_dynamic-update-slice_fusion.2
  389.4 1.4 bitcast_dynamic-update-slice_fusion.2
  391.5 1.4 bitcast_dynamic-update-slice_fusion.2
  395.1 39.3 %custom-call.33 = f32[4,128,128]{1,2,0:T(8,128)S(1)} custom-call(f32[4,128,128]{2,1,0:T(8,128)S(1)} %get-tuple-element.12), custom_call_target="InvertDiagBlocksLowerTriangular" | custom-call | tf_op jit(solution)/shard_map/triangular_solve | solution.py:58
  437.3 1.5 convolution_subtract_fusion.2
  (58 shorter events, 25.3 us)
Async XLA Ops:
  6.5 46.2 %all-gather.8.cloned.1.call-start = ((), (), s32[]{:S(2)}) async-start(), calls=%async_computation.3 | async-start | bytes 2621440 | tf_op jit(solution)/shard_map/all_gather | solution.py:11
  11.8 2.0 copy-start
  14.6 140.2 %reduce-scatter.2.cloned.1.call-start = ((), (), s32[]{:S(2)}) async-start(), calls=%async_computation.1 | async-start | bytes 9437184 | tf_op jit(solution)/shard_map/reduce_scatter | solution.py:51
  65.1 143.3 %all-gather.10.cloned.1.call-start = ((), (), s32[]{:S(2)}) async-start(), calls=%async_computation.4 | async-start | bytes 5242880 | tf_op jit(solution)/shard_map/all_gather | solution.py:11
  157.2 137.5 %all-gather.6.cloned.1.call-start = ((), (), s32[]{:S(2)}) async-start(), calls=%async_computation.2 | async-start | bytes 9437184 | tf_op jit(solution)/shard_map/all_gather | solution.py:55
  297.8 1.0 copy-start.1
Sparse Core Ops, SparseCore 0:
  14.8 37.8 all-gather.7
  65.2 89.5 reduce-scatter.1
  157.4 51.0 all-gather.9
  212.6 82.0 all-gather.5
